TPU v7x, 128 devices: a whole 4x4x4 slice. The times are simulated.
128 devices in a mesh: row: 8 (over x_hi, y), col: 16 (over z, x_lo, core).
Axes of the slice: x: 4 (x_hi: 2, x_lo: 2; x = x_hi * 2 + x_lo), y: 4, z: 4, core: 2. Of those that a mesh axis runs over, the one named last changes fastest.
Arguments:
- fields: bfloat16 [128, 128, 1024], P('row', 'col'), may hold values from -6 to 6
- cotangent: bfloat16 [128, 128, 1024], P('row', 'col'), may hold values from -6 to 6
- query_weight: bfloat16 [1024, 1024], P(('row', 'col')), may hold values from -1 to 6
- key_weight: bfloat16 [1024, 1024], P(('row', 'col')), may hold values from -1 to 6
- value_weight: bfloat16 [1024, 1024], P(('row', 'col')), may hold values from -0.1875 to 0.1875
- output_weight: bfloat16 [1024, 1024], P(('row', 'col')), may hold values from -0.1875 to 0.1875
- expert_ids: int32 [8, 16, 128, 2], P('row', 'col'), may hold values from 0 to 31, all different within a row; in each aligned block of 128 rows (0 to 127, 128 to 255, ..., all dimensions but the last counted through in order) at most 10 rows name the same one
- gate_values: float32 [8, 16, 128, 2], P('row', 'col'), may hold values from 0.2 to 1
- gate_weight: bfloat16 [128, 1024, 1024], P(('row', 'col')), may hold values from -0.1875 to 0.1875
- up_weight: bfloat16 [128, 1024, 1024], P(('row', 'col')), may hold values from -0.1875 to 0.1875
- down_weight: bfloat16 [128, 1024, 1024], P(('row', 'col')), may hold values from -0.09375 to 0.09375
Outputs:
- field_grad: bfloat16 [128, 128, 1024], P('row', 'col')
- gate_grad: bfloat16 [128, 1024, 1024], P(('row', 'col'))
- up_grad: bfloat16 [128, 1024, 1024], P(('row', 'col'))
- down_grad: bfloat16 [128, 1024, 1024], P(('row', 'col'))
Inputs may be any that keep to these rules, and one draw needn't show every extreme that they name: `expert_ids`: the 2 entries of a cell differ; among one device's 128 cells no expert is named more than 10 times, a bound that some block reaches.
All inputs are finite; a program needn't handle non-finite values.
Results may differ from a plain program's by a relative error of at most 0.0095.
Values may be sent and summed in bfloat16 or wider, within the bound.
No kernel may reach another device: no remote copies, remote signals or barrier semaphores. Data moves between devices by JAX's collectives and lax.ppermute only.
A program may use at most 192 MiB of HBM per device.

v0:
```python
import math
import jax
import jax.numpy as jnp
from jax import lax
from jax.sharding import PartitionSpec as P

HEADS = 16
EXPERTS = 32
CAP = 10
EPS = 1e-06


def normalize(values):
    scale = lax.rsqrt(jnp.mean(values * values, axis=-1, keepdims=True) + EPS)
    return (values * scale, scale)


def norm_back(grads, normed, scale):
    return scale * (grads - normed * jnp.mean(grads * normed, axis=-1, keepdims=True))


def contract_rows(left, right):
    return lax.dot_general(
        left, right, (((0,), (0,)), ((), ())), preferred_element_type=jnp.float32
    )


def times_transposed(left, right):
    return lax.dot_general(
        left, right, (((1,), (1,)), ((), ())), preferred_element_type=jnp.float32
    )


def attention_forward(normed_half, query_weight, key_weight, value_weight, output_weight):
    latitudes, longitudes, features = normed_half.shape
    head_size = features // HEADS
    flat_rows = normed_half.reshape(latitudes * longitudes, features)

    def project(weight):
        result = jnp.dot(flat_rows, weight, preferred_element_type=jnp.float32)
        return result.astype(jnp.bfloat16).reshape(latitudes, longitudes, HEADS, head_size)

    queries = project(query_weight)
    key_rows = project(key_weight)
    value_rows = project(value_weight)
    factor = 1.0 / math.sqrt(head_size)
    scores = (
        jnp.einsum("bqhd,bkhd->bhqk", queries, key_rows, preferred_element_type=jnp.float32)
        * factor
    )
    attention = jax.nn.softmax(scores, axis=-1)
    attention_half = attention.astype(jnp.bfloat16)
    attended = jnp.einsum(
        "bhqk,bkhd->bqhd", attention_half, value_rows, preferred_element_type=jnp.float32
    ).astype(jnp.bfloat16)
    mixture = jnp.dot(
        attended.reshape(latitudes * longitudes, features),
        output_weight,
        preferred_element_type=jnp.float32,
    )
    return (mixture, (queries, key_rows, value_rows, attention, attention_half))


def attention_backward(block_half, stored, query_weight, key_weight, value_weight, output_weight):
    queries, key_rows, value_rows, attention, attention_half = stored
    latitudes, longitudes, head_count, head_size = queries.shape
    features = head_count * head_size
    factor = 1.0 / math.sqrt(head_size)
    out_grad = times_transposed(block_half.reshape(-1, features), output_weight)
    out_grad = out_grad.astype(jnp.bfloat16).reshape(latitudes, longitudes, head_count, head_size)
    mass_grad = jnp.einsum(
        "bqhd,bkhd->bhqk", out_grad, value_rows, preferred_element_type=jnp.float32
    )
    score_grad = (
        attention * (mass_grad - jnp.sum(attention * mass_grad, axis=-1, keepdims=True)) * factor
    )
    score_grad = score_grad.astype(jnp.bfloat16)
    query_grad = jnp.einsum(
        "bhqk,bkhd->bqhd", score_grad, key_rows, preferred_element_type=jnp.float32
    ).astype(jnp.bfloat16)
    key_grad = jnp.einsum(
        "bhqk,bqhd->bkhd", score_grad, queries, preferred_element_type=jnp.float32
    ).astype(jnp.bfloat16)
    value_grad = jnp.einsum(
        "bhqk,bqhd->bkhd", attention_half, out_grad, preferred_element_type=jnp.float32
    ).astype(jnp.bfloat16)
    total = times_transposed(query_grad.reshape(-1, features), query_weight)
    total = total + times_transposed(key_grad.reshape(-1, features), key_weight)
    return total + times_transposed(value_grad.reshape(-1, features), value_weight)


def expert_terms(inputs, mix_grad, gate_block, up_block, down_block):
    gate_pre = jnp.dot(inputs, gate_block, preferred_element_type=jnp.float32)
    up_pre = jnp.dot(inputs, up_block, preferred_element_type=jnp.float32)
    sigmoid_gate = jax.nn.sigmoid(gate_pre)
    swish_gate = gate_pre * sigmoid_gate
    hidden = (swish_gate * up_pre).astype(jnp.bfloat16)
    hidden_grad = times_transposed(mix_grad, down_block)
    gate_delta = (
        hidden_grad * up_pre * sigmoid_gate * (1.0 + gate_pre * (1.0 - sigmoid_gate))
    ).astype(jnp.bfloat16)
    up_delta = (hidden_grad * swish_gate).astype(jnp.bfloat16)
    down_term = contract_rows(hidden, mix_grad).astype(jnp.bfloat16)
    gate_term = contract_rows(inputs, gate_delta).astype(jnp.bfloat16)
    up_term = contract_rows(inputs, up_delta).astype(jnp.bfloat16)
    returned = times_transposed(gate_delta, gate_block) + times_transposed(up_delta, up_block)
    return (gate_term, up_term, down_term, returned)


def assignment_slots(chosen):
    onehot = (chosen[:, None] == jnp.arange(EXPERTS, dtype=jnp.int32)[None, :]).astype(jnp.int32)
    before = jnp.cumsum(onehot, axis=0) - onehot
    return jnp.sum(before * onehot, axis=1)


def body(
    fields,
    cotangent,
    query_weight,
    key_weight,
    value_weight,
    output_weight,
    expert_ids,
    gate_values,
    gate_weight,
    up_weight,
    down_weight,
):
    field_rows, cotangent_rows = (
        lax.all_to_all(fields, "col", split_axis=0, concat_axis=1, tiled=True),
        lax.all_to_all(cotangent, "col", split_axis=0, concat_axis=1, tiled=True),
    )
    query_all, key_all, value_all, output_all = (
        lax.all_gather(query_weight, ("row", "col"), axis=0, tiled=True),
        lax.all_gather(key_weight, ("row", "col"), axis=0, tiled=True),
        lax.all_gather(value_weight, ("row", "col"), axis=0, tiled=True),
        lax.all_gather(output_weight, ("row", "col"), axis=0, tiled=True),
    )
    latitudes, longitudes, features = field_rows.shape
    token_count = latitudes * longitudes
    top_count = expert_ids.shape[-1]
    fields_full = field_rows.astype(jnp.float32)
    normed_in, scale_in = normalize(fields_full)
    normed_in_half = normed_in.astype(jnp.bfloat16)
    mixture, stored = attention_forward(normed_in_half, query_all, key_all, value_all, output_all)
    mid_stream = (fields_full.reshape(token_count, features) + mixture).astype(jnp.bfloat16)
    normed_mid, scale_mid = normalize(mid_stream.astype(jnp.float32))
    normed_mid_half = normed_mid.astype(jnp.bfloat16)
    chosen = expert_ids.reshape(token_count * top_count)
    slot_index = assignment_slots(chosen)
    places = chosen * CAP + slot_index
    cotangent_full = cotangent_rows.reshape(token_count, features).astype(jnp.float32)
    weights = gate_values.reshape(token_count, top_count)
    mix_grad = (
        (weights[:, :, None] * cotangent_full[:, None, :])
        .astype(jnp.bfloat16)
        .reshape(token_count * top_count, features)
    )
    inputs = jnp.broadcast_to(
        normed_mid_half[:, None, :], (token_count, top_count, features)
    ).reshape(token_count * top_count, features)
    blank_buffer = jnp.zeros((EXPERTS * CAP, features), jnp.bfloat16)
    send_inputs = blank_buffer.at[places].set(inputs)
    send_grads = blank_buffer.at[places].set(mix_grad)
    row_devices = lax.axis_size("row")
    col_devices = lax.axis_size("col")
    all_devices = row_devices * col_devices
    slice_count = all_devices // EXPERTS

    def spread(buffer):
        widened = jnp.broadcast_to(
            buffer.reshape(EXPERTS, 1, CAP, features), (EXPERTS, slice_count, CAP, features)
        )
        return widened.reshape(all_devices, CAP, features)

    recv_inputs, recv_grads = (
        lax.all_to_all(
            spread(send_inputs), ("row", "col"), split_axis=0, concat_axis=0, tiled=True
        ),
        lax.all_to_all(spread(send_grads), ("row", "col"), split_axis=0, concat_axis=0, tiled=True),
    )
    row_count = all_devices * CAP
    gate_term, up_term, down_term, returned = expert_terms(
        recv_inputs.reshape(row_count, features),
        recv_grads.reshape(row_count, features),
        gate_weight[0],
        up_weight[0],
        down_weight[0],
    )
    coming_back = lax.all_to_all(
        returned.reshape(all_devices, CAP, features).astype(jnp.bfloat16),
        ("row", "col"),
        split_axis=0,
        concat_axis=0,
        tiled=True,
    ).astype(jnp.float32)
    summed = jnp.sum(coming_back.reshape(EXPERTS, slice_count, CAP, features), axis=1)
    gathered = summed.reshape(EXPERTS * CAP, features)[places]
    normed_grad = jnp.sum(gathered.reshape(token_count, top_count, features), axis=1)
    block_grad = cotangent_full + norm_back(normed_grad, normed_mid, scale_mid)
    block_half = block_grad.astype(jnp.bfloat16)
    branch_grad = attention_backward(
        block_half.reshape(latitudes, longitudes, features),
        stored,
        query_all,
        key_all,
        value_all,
        output_all,
    )
    field_total = block_grad + norm_back(
        branch_grad, normed_in.reshape(token_count, features), scale_in.reshape(token_count, 1)
    )
    field_half = field_total.astype(jnp.bfloat16).reshape(latitudes, longitudes, features)
    field_grad = lax.all_to_all(field_half, "col", split_axis=1, concat_axis=0, tiled=True)
    return (field_grad, gate_term[None], up_term[None], down_term[None])


def solution(mesh):
    in_specs = (
        P("row", "col", None),
        P("row", "col", None),
        P(("row", "col"), None),
        P(("row", "col"), None),
        P(("row", "col"), None),
        P(("row", "col"), None),
        P("row", "col", None, None),
        P("row", "col", None, None),
        P(("row", "col"), None, None),
        P(("row", "col"), None, None),
        P(("row", "col"), None, None),
    )
    out_specs = (
        P("row", "col", None),
        P(("row", "col"), None, None),
        P(("row", "col"), None, None),
        P(("row", "col"), None, None),
    )
    return jax.shard_map(body, mesh=mesh, in_specs=in_specs, out_specs=out_specs, check_vma=False)
```

profile of v0, /device:TPU:1, one launch (start us, length us, event | category | flops | bytes accessed | tf_op | source)
XLA Modules:
  0.0 1054.5 jit_solution(7280352464968909564)
XLA Ops:
  7.2 0.7 all-gather.7.cloned.1.call-update
  8.0 0.7 all-gather.9.cloned.1.call-update
  8.7 0.7 all-gather.5.cloned.1.call-update
  10.0 7.8 all-to-all-start
  17.7 0.8 copy.59
  18.7 0.7 broadcast_multiply_fusion
  19.8 0.6 reduce-window.6
  20.7 4.3 all-to-all-done
  24.9 4.2 all-to-all-start.1
  29.2 0.8 copy.62
  30.2 1.3 mul.151
  31.5 1.9 mul.152
  33.5 2.6 scatter_custom_fusion
  36.0 1.3 broadcast_in_dim.19
  37.3 2.5 broadcast_in_dim.20
  39.8 9.7 all-to-all-start.2
  49.8 195.3 %all-gather.7.cloned.1.call-done = bf16[1024,1024]{1,0:T(8,128)(2,1)} async-done(((bf16[8,1024]{1,0:T(8,128)(2,1)}), bf16[1024,1024]{1,0:T(8,128)(2,1)}) %all-gather.7.cloned.1.call-update) | async-done | bytes 2097168 | tf_op jit(solution)/shard_map/all_gather | solution.py:134
  245.1 2.1 convolution_convert_fusion.6
  247.4 193.8 %all-gather.9.cloned.1.call-done = bf16[1024,1024]{1,0:T(8,128)(2,1)} async-done(((bf16[8,1024]{1,0:T(8,128)(2,1)}), bf16[1024,1024]{1,0:T(8,128)(2,1)}) %all-gather.9.cloned.1.call-update) | async-done | bytes 2097168 | tf_op jit(solution)/shard_map/all_gather | solution.py:135
  441.2 2.1 convolution_convert_fusion.5
  443.4 193.8 %all-gather.5.cloned.1.call-done = bf16[1024,1024]{1,0:T(8,128)(2,1)} async-done(((bf16[8,1024]{1,0:T(8,128)(2,1)}), bf16[1024,1024]{1,0:T(8,128)(2,1)}) %all-gather.5.cloned.1.call-update) | async-done | bytes 2097168 | tf_op jit(solution)/shard_map/all_gather | solution.py:136
  637.2 2.1 convolution_convert_fusion.7
  639.5 1.5 fusion.61
  641.0 1.4 convolution_convert_fusion.4
  642.4 190.7 %all-gather.11.cloned.1.call-done = bf16[1024,1024]{1,0:T(8,128)(2,1)} async-done(((bf16[8,1024]{1,0:T(8,128)(2,1)}), bf16[1024,1024]{1,0:T(8,128)(2,1)}) %all-gather.11.cloned.1.call-update) | async-done | bytes 2097168 | tf_op jit(solution)/shard_map/all_gather | solution.py:137
  833.1 2.2 multiply_reduce_fusion.2
  835.8 1.0 reshape.322
  836.8 2.4 scatter_custom_fusion.1
  839.1 1.2 broadcast_in_dim.22
  840.3 3.7 broadcast_in_dim.23
  844.0 8.2 all-to-all-start.3
  852.3 6.2 reshape.285
  858.5 46.5 %all-to-all-done.3 = bf16[128,10,1024]{2,1,0:T(8,128)(2,1)} async-done(((bf16[128,10,1024]{2,1,0:T(8,128)(2,1)}), bf16[128,10,1024]{2,1,0:T(8,128)(2,1)}, u32[]{:S(2)}, u32[]{:S(2)}) %all-to-all-start.3) | async-done | bytes 2621472 | tf_op jit(solution)/shard_map/all_to_all | solution.py:177
  905.0 6.1 reshape.288
  911.1 5.4 fusion.6
  916.6 2.9 fusion.9
  919.5 0.7 copy-done.9
  920.2 5.9 multiply_convert_fusion.1
  926.1 2.9 fusion.4
  929.1 4.4 add_convert_fusion
  933.4 6.0 convert_element_type.163
  939.4 6.7 all-to-all-start.4
  946.1 6.9 convert_bitcast_fusion.1
  953.1 8.6 convert_bitcast_fusion
  961.6 37.4 %all-to-all-done.4 = bf16[128,10,1024]{2,1,0:T(8,128)(2,1)} async-done(((bf16[128,10,1024]{2,1,0:T(8,128)(2,1)}), bf16[128,10,1024]{2,1,0:T(8,128)(2,1)}, u32[]{:S(2)}, u32[]{:S(2)}) %all-to-all-start.4) | async-done | bytes 2621472 | tf_op jit(solution)/shard_map/all_to_all | solution.py:190
  999.0 4.7 convert_reduce_fusion
  1003.8 1.8 reshape.291
  1005.6 2.0 gather_fusion
  1007.6 3.0 reshape.292
  1010.6 2.5 reduce_sum.89
  1013.3 2.5 convolution_convert_fusion.3
  1015.8 1.1 copy.63
  1017.0 2.6 convolution_convert_fusion
  1019.9 1.0 copy-done.11
  1020.9 2.7 convolution_convert_fusion.2
  1023.6 3.6 convolution_convert_fusion.1
  1027.2 1.9 fusion.63
  1029.1 0.8 convolution_add_fusion.1
  1030.0 0.9 fusion.30
  1032.2 2.1 reduce.12
  1034.4 0.9 reshape.331
  1035.2 4.3 all-to-all-start.5
  1039.5 6.9 convert_bitcast_fusion.2
  1046.9 0.8 copy.77
  (90 shorter events, 5.2 us)
Async XLA Ops:
  7.2 912.3 %copy-start = (bf16[1,1024,1024]{2,1,0:T(8,128)(2,1)S(1)}, bf16[1,1024,1024]{2,1,0:T(8,128)(2,1)}, u32[]{:S(2)}) copy-start(bf16[1,1024,1024]{2,1,0:T(8,128)(2,1)} %param.21) | copy-start | bytes 6291460
  7.2 237.9 %all-gather.7.cloned.1.call-start = ((), (), s32[]{:S(2)}) async-start(), calls=%async_computation.7 | async-start | bytes 2113536 | tf_op jit(solution)/shard_map/all_gather | solution.py:134
  7.9 433.3 %all-gather.9.cloned.1.call-start = ((), (), s32[]{:S(2)}) async-start(), calls=%async_computation.8 | async-start | bytes 2113536 | tf_op jit(solution)/shard_map/all_gather | solution.py:135
  8.7 628.6 %all-gather.5.cloned.1.call-start = ((), (), s32[]{:S(2)}) async-start(), calls=%async_computation.6 | async-start | bytes 2113536 | tf_op jit(solution)/shard_map/all_gather | solution.py:136
  9.4 823.7 %all-gather.11.cloned.1.call-start = ((), (), s32[]{:S(2)}) async-start(), calls=%async_computation.9 | async-start | bytes 2113536 | tf_op jit(solution)/shard_map/all_gather | solution.py:137
  10.0 15.0 %all-to-all-start = ((bf16[16,8,1024]{2,1,0:T(8,128)(2,1)}), bf16[16,8,1024]{2,1,0:T(8,128)(2,1)S(1)}, u32[]{:S(2)}, u32[]{:S(2)}) async-start(bf16[16,8,1024]{2,1,0:T(8,128)(2,1)} %param.12), calls=%async_computation | async-start | bytes 524288 | tf_op jit(solution)/shard_map/all_to_all | solution.py:131
  24.9 5.2 copy-start.6
  24.9 12.4 %all-to-all-start.1 = ((bf16[16,8,1024]{2,1,0:T(8,128)(2,1)}), bf16[16,8,1024]{2,1,0:T(8,128)(2,1)S(1)}, u32[]{:S(2)}, u32[]{:S(2)}) async-start(bf16[16,8,1024]{2,1,0:T(8,128)(2,1)} %param.11), calls=%async_computation.1 | async-start | bytes 524288 | tf_op jit(solution)/shard_map/all_to_all | solution.py:130
  39.8 800.5 %all-to-all-start.2 = ((bf16[128,10,1024]{2,1,0:T(8,128)(2,1)}), bf16[128,10,1024]{2,1,0:T(8,128)(2,1)}, u32[]{:S(2)}, u32[]{:S(2)}) async-start(bf16[128,10,1024]{2,1,0:T(8,128)(2,1)} %bitcast.161), calls=%async_computation.2 | async-start | bytes 8388608 | tf_op jit(solution)/shard_map/all_to_all | solution.py:180
  247.4 393.6 %copy-start.14 = (bf16[128,1024]{0,1:T(8,128)(2,1)}, bf16[128,1024]{0,1:T(8,128)(2,1)S(1)}, u32[]{:S(2)}) copy-start(bf16[128,1024]{0,1:T(8,128)(2,1)S(1)} %copy.55) | copy-start | bytes 786436
  443.4 198.9 %copy-start.15 = (bf16[128,1024]{0,1:T(8,128)(2,1)}, bf16[128,1024]{0,1:T(8,128)(2,1)S(1)}, u32[]{:S(2)}) copy-start(bf16[128,1024]{0,1:T(8,128)(2,1)S(1)} %copy.56) | copy-start | bytes 786436
  639.5 2.9 copy-start.12
  641.0 1.4 copy-start.21
  844.0 60.9 %all-to-all-start.3 = ((bf16[128,10,1024]{2,1,0:T(8,128)(2,1)}), bf16[128,10,1024]{2,1,0:T(8,128)(2,1)}, u32[]{:S(2)}, u32[]{:S(2)}) async-start(bf16[128,10,1024]{2,1,0:T(8,128)(2,1)} %bitcast.162), calls=%async_computation.3 | async-start | bytes 8388608 | tf_op jit(solution)/shard_map/all_to_all | solution.py:177
  911.1 5.4 copy-start.8
  911.1 5.4 copy-start.20
  916.5 2.9 copy-start.23
  916.6 3.6 copy-start.9
  920.2 5.9 copy-start.24
  920.2 5.9 copy-start.19
  926.1 2.9 copy-start.25
  926.1 3.0 copy-start.26
  939.4 59.6 %all-to-all-start.4 = ((bf16[128,10,1024]{2,1,0:T(8,128)(2,1)}), bf16[128,10,1024]{2,1,0:T(8,128)(2,1)}, u32[]{:S(2)}, u32[]{:S(2)}) async-start(bf16[128,10,1024]{2,1,0:T(8,128)(2,1)} %convert_element_type.163), calls=%async_computation.4 | async-start | bytes 8388608 | tf_op jit(solution)/shard_map/all_to_all | solution.py:190
  946.1 6.9 copy-start.10
  1007.6 5.7 copy-start.5
  1013.1 3.8 copy-start.22
  1016.9 2.6 copy-start.13
  1017.0 3.9 copy-start.16
  1019.9 1.0 copy-start.11
  1023.6 3.6 copy-start.2
  1027.2 2.0 copy-start.3
  1027.2 2.0 copy-start.18
  1027.2 2.8 copy-start.4
  1027.2 2.8 copy-start.17
  1030.0 1.0 copy-start.7
  1035.2 11.4 %all-to-all-start.5 = ((bf16[16,2,4096]{2,1,0:T(2,128)(2,1)}), bf16[16,2,4096]{2,1,0:T(2,128)(2,1)S(1)}, u32[]{:S(2)}, u32[]{:S(2)}) async-start(bf16[16,2,4096]{2,1,0:T(2,128)(2,1)} %reshape.331), calls=%async_computation.5 | async-start | bytes 524288 | tf_op jit(solution)/shard_map/all_to_all | solution.py:214
  1039.5 8.2 copy-start.1
Sparse Core Ops, SparseCore 0:
  9.7 235.3 all-gather.6
  246.8 194.2 all-gather.8
  442.9 194.2 all-gather.4
  638.8 194.2 all-gather.10
where the time goes:
time: 1060 us; the launch traced here: 1050 us
  waiting for transfers between devices  865 us (82%)
  matrix products  70.7 us (7%)
  local copies, waits for them, and re-layouts  49.5 us (5%)
  starting transfers between devices  41.1 us (4%)
  between operations  14.6 us (1%)
  other arithmetic  14.2 us (1%)
    all_gather x1, waiting for transfers between devices, body(): lax.all_gather(query_weight, ('row', 'col'), axis=0, tiled=True)  195 us
    all_gather x1, waiting for transfers between devices, body(): lax.all_gather(key_weight, ('row', 'col'), axis=0, tiled=True)  194 us
    all_gather x1, waiting for transfers between devices, body(): lax.all_gather(value_weight, ('row', 'col'), axis=0, tiled=True)  194 us
    all_gather x1, waiting for transfers between devices, body(): lax.all_gather(output_weight, ('row', 'col'), axis=0, tiled=True)  191 us
    all_to_all x1, waiting for transfers between devices, body(): lax.all_to_all(spread(send_inputs), ('row', 'col'), split_axis=0, concat_...  46.5 us
    all_to_all x1, waiting for transfers between devices, body(): lax.all_to_all(returned.reshape(all_devices, CAP, features).astype(jnp.bf...  37.4 us
    dot_general x3, matrix products, contract_rows(): lax.dot_general(left, right, (((0,), (0,)), ((), ())), preferred_element_...  22.5 us
  transfers between devices with their start and end apart: 10, of which 8 were waited for; matrix products, arithmetic and copies ran while one was open for 6% of the time, Pallas kernels for 0%

commit v1 on v0

--- a/solution.py
+++ b/solution.py
@@ -134,7 +134,12 @@
         lax.all_gather(query_weight, ("row", "col"), axis=0, tiled=True),
         lax.all_gather(key_weight, ("row", "col"), axis=0, tiled=True),
         lax.all_gather(value_weight, ("row", "col"), axis=0, tiled=True),
-        lax.all_gather(output_weight, ("row", "col"), axis=0, tiled=True),
+        jnp.concatenate(
+            lax.all_to_all(
+                jnp.stack([output_weight] * lax.axis_size(("row", "col"))), ("row", "col"), 0, 0
+            ),
+            axis=0,
+        ),
     )
     latitudes, longitudes, features = field_rows.shape
     token_count = latitudes * longitudes

time: 1060 us -> 882 us (0.83)
  waiting for transfers between devices: 865 us -> 668 us
  blocking collectives: 0 us -> 26.4 us
    all_gather x1 -> x0, waiting for transfers between devices: 191 us -> none  [body(): lax.all_gather(output_weight, ('row', 'col'), axis=0, tiled=True)]
    all_to_all x0 -> x2, blocking collectives: none -> 26.4 us  [the longest x1 14.9 us: body(): lax.all_to_all(fields, 'col', split_axis=0, concat_axis=1, tiled=True)]
    all_gather x1, waiting for transfers between devices: 195 us -> 172 us  [body(): lax.all_gather(query_weight, ('row', 'col'), axis=0, tiled=True)]
    all_to_all x2 -> x1, waiting for transfers between devices: 4.25 us -> 21.9 us  [body(): lax.all_to_all(jnp.stack([output_weight] * lax.axis_size(('row', 'col')))...]
  transfers between devices with their start and end apart: 10 -> 8, of which waited for: 8 -> 7; matrix products, arithmetic and copies ran while one was open for 6% -> 7% of each run, Pallas kernels for 0% -> 0%
where the time goes in v1:
time: 882 us; the launch traced here: 872 us
  waiting for transfers between devices  668 us (76%)
  matrix products  69.5 us (8%)
  local copies, waits for them, and re-layouts  48.4 us (5%)
  starting transfers between devices  32.6 us (4%)
  blocking collectives  26.4 us (3%)
  between operations  14.8 us (2%)
  other arithmetic  12.3 us (1%)
    all_gather x1, waiting for transfers between devices, body(): lax.all_gather(value_weight, ('row', 'col'), axis=0, tiled=True)  194 us
    all_gather x1, waiting for transfers between devices, body(): lax.all_gather(key_weight, ('row', 'col'), axis=0, tiled=True)  194 us
    all_gather x1, waiting for transfers between devices, body(): lax.all_gather(query_weight, ('row', 'col'), axis=0, tiled=True)  172 us
    all_to_all x1, waiting for transfers between devices, body(): lax.all_to_all(spread(send_inputs), ('row', 'col'), split_axis=0, concat_...  46.8 us
    all_to_all x1, waiting for transfers between devices, body(): lax.all_to_all(returned.reshape(all_devices, CAP, features).astype(jnp.bf...  37.4 us
    dot_general x3, matrix products, contract_rows(): lax.dot_general(left, right, (((0,), (0,)), ((), ())), preferred_element_...  22.5 us
    all_to_all x1, waiting for transfers between devices, body(): lax.all_to_all(jnp.stack([output_weight] * lax.axis_size(('row', 'col')))...  21.9 us
    dot_general x7, matrix products, times_transposed(): lax.dot_general(left, right, (((1,), (1,)), ((), ())), preferred_element_...  19.3 us
  transfers between devices with their start and end apart: 8, of which 7 were waited for; matrix products, arithmetic and copies ran while one was open for 7% of the time, Pallas kernels for 0%

profile of v1, /device:TPU:1, one launch (start us, length us, event | category | flops | bytes accessed | tf_op | source)
XLA Modules:
  0.0 872.3 jit_solution(7459040680034971941)
XLA Ops:
  7.2 0.7 all-gather.6.cloned.1.call-update
  8.0 0.7 all-gather.8.cloned.1.call-update
  8.7 0.7 all-gather.4.cloned.1.call-update
  9.4 14.9 %all_to_all.50 = bf16[16,8,1024]{2,1,0:T(8,128)(2,1)S(1)} all-to-all(bf16[16,8,1024]{2,1,0:T(8,128)(2,1)} %param.11), channel_id=1, replica_groups=mesh['row'=8,'col'=16] {'col'}, dimensions={0} | all-to-all | bytes 524288 | tf_op jit(solution)/shard_map/all_to_all | solution.py:130
  24.3 11.5 %all_to_all.51 = bf16[16,8,1024]{2,1,0:T(8,128)(2,1)S(1)} all-to-all(bf16[16,8,1024]{2,1,0:T(8,128)(2,1)} %param.12), channel_id=1, replica_groups=mesh['row'=8,'col'=16] {'col'}, dimensions={0} | all-to-all | bytes 524288 | tf_op jit(solution)/shard_map/all_to_all | solution.py:131
  35.8 2.3 stack.2
  38.1 8.1 all-to-all-start.2
  46.9 0.6 reduce-window.6
  48.2 1.3 mul.151
  49.5 1.9 mul.152
  51.4 2.6 scatter_custom_fusion
  54.0 1.3 broadcast_in_dim.19
  55.3 21.9 %all-to-all-done.2 = bf16[128,8,1024]{2,1,0:T(8,128)(2,1)} async-done(((bf16[128,8,1024]{2,1,0:T(8,128)(2,1)}), bf16[128,8,1024]{2,1,0:T(8,128)(2,1)}, u32[]{:S(2)}, u32[]{:S(2)}) %all-to-all-start.2) | async-done | bytes 2097184 | tf_op jit(solution)/shard_map/all_to_all | solution.py:138
  77.2 2.5 broadcast_in_dim.20
  79.7 5.8 all-to-all-start.3
  85.7 172.4 %all-gather.6.cloned.1.call-done = bf16[1024,1024]{1,0:T(8,128)(2,1)} async-done(((bf16[8,1024]{1,0:T(8,128)(2,1)}), bf16[1024,1024]{1,0:T(8,128)(2,1)}) %all-gather.6.cloned.1.call-update) | async-done | bytes 2097168 | tf_op jit(solution)/shard_map/all_gather | solution.py:134
  258.2 2.1 convolution_convert_fusion.5
  260.4 193.8 %all-gather.8.cloned.1.call-done = bf16[1024,1024]{1,0:T(8,128)(2,1)} async-done(((bf16[8,1024]{1,0:T(8,128)(2,1)}), bf16[1024,1024]{1,0:T(8,128)(2,1)}) %all-gather.8.cloned.1.call-update) | async-done | bytes 2097168 | tf_op jit(solution)/shard_map/all_gather | solution.py:135
  454.2 2.1 convolution_convert_fusion.4
  456.5 193.8 %all-gather.4.cloned.1.call-done = bf16[1024,1024]{1,0:T(8,128)(2,1)} async-done(((bf16[8,1024]{1,0:T(8,128)(2,1)}), bf16[1024,1024]{1,0:T(8,128)(2,1)}) %all-gather.4.cloned.1.call-update) | async-done | bytes 2097168 | tf_op jit(solution)/shard_map/all_gather | solution.py:136
  650.2 2.1 convolution_convert_fusion.6
  652.5 1.5 fusion.75
  654.0 1.4 convolution_convert_fusion.3
  655.4 2.2 multiply_reduce_fusion.2
  658.0 1.0 reshape.328
  659.0 2.4 scatter_custom_fusion.1
  661.4 1.2 broadcast_in_dim.22
  662.6 3.7 broadcast_in_dim.23
  666.3 7.5 all-to-all-start.4
  673.9 6.2 reshape.291
  680.0 46.8 %all-to-all-done.4 = bf16[128,10,1024]{2,1,0:T(8,128)(2,1)} async-done(((bf16[128,10,1024]{2,1,0:T(8,128)(2,1)}), bf16[128,10,1024]{2,1,0:T(8,128)(2,1)}, u32[]{:S(2)}, u32[]{:S(2)}) %all-to-all-start.4) | async-done | bytes 2621472 | tf_op jit(solution)/shard_map/all_to_all | solution.py:182
  726.8 6.1 reshape.294
  733.0 5.4 fusion.6
  738.4 2.9 fusion.9
  741.3 0.7 copy-done.9
  742.0 5.9 multiply_convert_fusion.1
  748.0 2.9 fusion.4
  750.9 4.4 add_convert_fusion
  755.3 5.9 convert_element_type.163
  761.2 6.7 all-to-all-start.5
  768.0 6.9 convert_bitcast_fusion.1
  774.9 8.6 convert_bitcast_fusion
  783.5 37.4 %all-to-all-done.5 = bf16[128,10,1024]{2,1,0:T(8,128)(2,1)} async-done(((bf16[128,10,1024]{2,1,0:T(8,128)(2,1)}), bf16[128,10,1024]{2,1,0:T(8,128)(2,1)}, u32[]{:S(2)}, u32[]{:S(2)}) %all-to-all-start.5) | async-done | bytes 2621472 | tf_op jit(solution)/shard_map/all_to_all | solution.py:195
  820.9 4.7 convert_reduce_fusion
  825.7 1.9 reshape.297
  827.5 2.0 gather_fusion
  829.6 1.9 reshape.298
  831.4 1.2 reduce_sum.89
  832.9 2.4 fusion.26
  835.6 1.5 convolution_convert_fusion
  837.1 0.4 fusion.76
  837.4 1.0 copy-done.11
  838.4 2.7 convolution_convert_fusion.2
  841.1 3.6 convolution_convert_fusion.1
  844.8 1.9 fusion.77
  846.7 0.8 convolution_add_fusion.1
  847.6 0.9 fusion.44
  848.8 0.4 copy.78
  849.2 0.5 broadcast.164
  849.7 2.1 reduce.12
  851.9 0.9 reshape.337
  852.8 4.3 all-to-all-start.6
  857.1 6.9 convert_bitcast_fusion.2
  864.5 0.8 copy.77
  (96 shorter events, 3.7 us)
Async XLA Ops:
  7.2 734.2 %copy-start = (bf16[1,1024,1024]{2,1,0:T(8,128)(2,1)S(1)}, bf16[1,1024,1024]{2,1,0:T(8,128)(2,1)}, u32[]{:S(2)}) copy-start(bf16[1,1024,1024]{2,1,0:T(8,128)(2,1)} %param.21) | copy-start | bytes 6291460
  7.2 251.0 %all-gather.6.cloned.1.call-start = ((), (), s32[]{:S(2)}) async-start(), calls=%async_computation.8 | async-start | bytes 2113536 | tf_op jit(solution)/shard_map/all_gather | solution.py:134
  7.9 446.3 %all-gather.8.cloned.1.call-start = ((), (), s32[]{:S(2)}) async-start(), calls=%async_computation.9 | async-start | bytes 2113536 | tf_op jit(solution)/shard_map/all_gather | solution.py:135
  8.7 641.6 %all-gather.4.cloned.1.call-start = ((), (), s32[]{:S(2)}) async-start(), calls=%async_computation.7 | async-start | bytes 2113536 | tf_op jit(solution)/shard_map/all_gather | solution.py:136
  35.8 12.3 %copy-start.5 = (bf16[16,8,1024]{2,1,0:T(8,128)(2,1)}, bf16[16,8,1024]{2,1,0:T(8,128)(2,1)S(1)}, u32[]{:S(2)}) copy-start(bf16[16,8,1024]{2,1,0:T(8,128)(2,1)S(1)} %all_to_all.51) | copy-start | bytes 786436
  38.1 8.1 copy-start.21
  38.1 9.6 %copy-start.22 = (f32[1,1,128,2]{2,3,1,0:T(2,128)S(1)}, f32[1,1,128,2]{2,3,1,0:T(2,128)}, u32[]{:S(2)}) copy-start(f32[1,1,128,2]{2,3,1,0:T(2,128)} %param.18) | copy-start | bytes 3076
  38.1 39.0 %all-to-all-start.2 = ((bf16[128,8,1024]{2,1,0:T(8,128)(2,1)}), bf16[128,8,1024]{2,1,0:T(8,128)(2,1)}, u32[]{:S(2)}, u32[]{:S(2)}) async-start(bf16[128,8,1024]{2,1,0:T(8,128)(2,1)} %stack.2), calls=%async_computation.2 | async-start | bytes 4194304 | tf_op jit(solution)/shard_map/all_to_all | solution.py:138
  79.7 582.9 %all-to-all-start.3 = ((bf16[128,10,1024]{2,1,0:T(8,128)(2,1)}), bf16[128,10,1024]{2,1,0:T(8,128)(2,1)}, u32[]{:S(2)}, u32[]{:S(2)}) async-start(bf16[128,10,1024]{2,1,0:T(8,128)(2,1)} %bitcast.174), calls=%async_computation.3 | async-start | bytes 8388608 | tf_op jit(solution)/shard_map/all_to_all | solution.py:185
  260.4 393.6 %copy-start.14 = (bf16[128,1024]{0,1:T(8,128)(2,1)}, bf16[128,1024]{0,1:T(8,128)(2,1)S(1)}, u32[]{:S(2)}) copy-start(bf16[128,1024]{0,1:T(8,128)(2,1)S(1)} %copy.55) | copy-start | bytes 786436
  456.4 198.9 %copy-start.16 = (bf16[128,1024]{0,1:T(8,128)(2,1)}, bf16[128,1024]{0,1:T(8,128)(2,1)S(1)}, u32[]{:S(2)}) copy-start(bf16[128,1024]{0,1:T(8,128)(2,1)S(1)} %copy.56) | copy-start | bytes 786436
  652.5 2.9 copy-start.12
  654.0 1.4 copy-start.25
  666.3 60.5 %all-to-all-start.4 = ((bf16[128,10,1024]{2,1,0:T(8,128)(2,1)}), bf16[128,10,1024]{2,1,0:T(8,128)(2,1)}, u32[]{:S(2)}, u32[]{:S(2)}) async-start(bf16[128,10,1024]{2,1,0:T(8,128)(2,1)} %bitcast.175), calls=%async_computation.4 | async-start | bytes 8388608 | tf_op jit(solution)/shard_map/all_to_all | solution.py:182
  733.0 5.4 copy-start.8
  733.0 5.4 copy-start.24
  738.4 2.9 copy-start.27
  738.4 3.6 copy-start.9
  742.0 5.9 copy-start.28
  742.0 5.9 copy-start.23
  748.0 2.9 copy-start.29
  748.0 3.0 copy-start.30
  761.2 59.7 %all-to-all-start.5 = ((bf16[128,10,1024]{2,1,0:T(8,128)(2,1)}), bf16[128,10,1024]{2,1,0:T(8,128)(2,1)}, u32[]{:S(2)}, u32[]{:S(2)}) async-start(bf16[128,10,1024]{2,1,0:T(8,128)(2,1)} %convert_element_type.163), calls=%async_computation.5 | async-start | bytes 8388608 | tf_op jit(solution)/shard_map/all_to_all | solution.py:195
  768.0 6.9 copy-start.10
  829.6 3.4 copy-start.6
  832.7 2.9 copy-start.15
  832.7 2.9 copy-start.17
  832.7 2.9 copy-start.26
  835.6 1.5 copy-start.13
  835.6 2.8 copy-start.18
  837.4 1.0 copy-start.11
  841.1 3.6 copy-start.2
  844.7 2.0 copy-start.3
  844.7 2.0 copy-start.20
  844.7 2.8 copy-start.4
  844.7 2.8 copy-start.19
  847.5 1.0 copy-start.7
  852.8 11.4 %all-to-all-start.6 = ((bf16[16,2,4096]{2,1,0:T(2,128)(2,1)}), bf16[16,2,4096]{2,1,0:T(2,128)(2,1)S(1)}, u32[]{:S(2)}, u32[]{:S(2)}) async-start(bf16[16,2,4096]{2,1,0:T(2,128)(2,1)} %reshape.337), calls=%async_computation.6 | async-start | bytes 524288 | tf_op jit(solution)/shard_map/all_to_all | solution.py:219
  857.1 8.2 copy-start.1
Sparse Core Ops, SparseCore 0:
  9.7 248.3 all-gather.5
  259.9 194.2 all-gather.7
  455.9 194.2 all-gather.3
